TPU v7x, 32 devices: a whole 2x2x4 slice. The times are simulated.
32 devices in a mesh: row: 8 (over y, x, core), col: 4 (over z).
Axes of the slice: x: 2, y: 2, z: 4, core: 2. Of those that a mesh axis runs over, the one named last changes fastest.
Arguments:
- positions: float32 [3, 32768], P(None, ('row', 'col')), may hold values from 0 to 1
- segments: float32 [3, 32768], P(None, ('row', 'col')), may hold values from -1.2 to 1.2
- radius: float32 [32768], P(('row', 'col')), may hold values from 0.05 to 0.2
- currents: float32 [2, 32768], P(None, ('row', 'col')), may hold values from -6 to 6
- resist: float32 [32768], P(('row', 'col')), may hold values from 0.3 to 3
- slot_of: int32 [32768], P(('row', 'col')), may hold values from 0 to 1023, as said below
- pair_list: int32 [1024, 2], P(('row', 'col')), may hold values from 0 to 63, as said below
- near_flag: int32 [1024], P(('row', 'col')), may hold values from 0 to 2, as said below
Outputs:
- voltage: float32 [2, 32768], P(None, ('row', 'col'))
Inputs may be any that keep to these rules, and one draw needn't show every extreme that they name: `slot_of`: the elements of shard d hold the values 0 to 1023 once each; a value s puts the element in cluster d * 2 + s // 512. `pair_list`: shard d = r * 4 + c lists 32 slots; each live slot holds a pair (I, J) with I <= J, I in clusters r * 2 * 4 to (r + 1) * 2 * 4 - 1 and (J // 2) % 4 = c; a pair stands in one live slot at most, over all shards. Empty slots hold I = r * 2 * 4 and J = c * 2. `near_flag`: 0 marks an empty slot.
All inputs are finite; a program needn't handle non-finite values.
Results may differ from a plain program's by a relative error of at most 0.0003.
Values sent between devices are 32-bit elements; how exact they have to be, the bound alone decides.
A program may use at most 64 MiB of HBM per device.

v0:
```python
import math

import jax
import jax.numpy as jnp
from jax import lax
from jax.sharding import PartitionSpec as P

CS = 512


gauss_step = 0.5 / math.sqrt(3.0)
kernel_gain = 0.25
group_size = 4


def partner(block, axis, distance):
    count = lax.axis_size(axis)
    route = []
    for low in range(count):
        high = low | 1 << distance
        if high != low and high < count:
            route += [(low, high), (high, low)]
    return lax.ppermute(block, axis, route)


def tile_block(
    points_first, vectors_first, radii_first, points_second, vectors_second, radii_second, is_near
):
    softening = radii_first[:, None] ** 2 + radii_second[None, :] ** 2
    alignment = vectors_first[0][:, None] * vectors_second[0][None, :]
    for component in (1, 2):
        alignment = (
            alignment + vectors_first[component][:, None] * vectors_second[component][None, :]
        )

    def far_part():
        squared = softening
        for component in range(3):
            squared = (
                squared
                + (points_first[component][:, None] - points_second[component][None, :]) ** 2
            )
        return 1.0 / jnp.sqrt(squared)

    def near_part():
        summed = jnp.zeros_like(softening)
        for sign_first in (-1.0, 1.0):
            for sign_second in (-1.0, 1.0):
                squared = softening
                for component in range(3):
                    moved_first = (
                        points_first[component] + sign_first * gauss_step * vectors_first[component]
                    )
                    moved_second = (
                        points_second[component]
                        + sign_second * gauss_step * vectors_second[component]
                    )
                    squared = squared + (moved_first[:, None] - moved_second[None, :]) ** 2
                summed = summed + 1.0 / jnp.sqrt(squared)
        return 0.25 * summed

    inverse = lax.cond(is_near, near_part, far_part)
    return kernel_gain * alignment * inverse


def slot_terms(block_first, block_second, flag_value, diagonal_pair):
    step_rows = min(128, CS)

    def live_terms():
        is_near = flag_value == 2
        rows_out = []
        mirror_sum = jnp.zeros((2, CS), jnp.float32)
        for offset in range(0, CS, step_rows):
            portion = block_first[:, offset : offset + step_rows]
            kernel_tile = tile_block(
                portion[0:3],
                portion[3:6],
                portion[6],
                block_second[0:3],
                block_second[3:6],
                block_second[6],
                is_near,
            )
            rows_out.append(
                jnp.dot(block_second[7:9], kernel_tile.T, precision=lax.Precision.HIGHEST)
            )
            mirror_sum = mirror_sum + jnp.dot(
                portion[7:9], kernel_tile, precision=lax.Precision.HIGHEST
            )
        mirror_weight = 1.0 - diagonal_pair.astype(jnp.float32)
        return (jnp.concatenate(rows_out, 1), mirror_weight * mirror_sum)

    def empty_terms():
        blank = jnp.zeros((2, CS), jnp.float32)
        return (blank, blank)

    return lax.cond(flag_value > 0, live_terms, empty_terms)


def on_device(positions, segments, radius, currents, resist, slot_of, pair_list, near_flag):
    local_count = positions.shape[1]
    packed = jnp.concatenate([positions, segments, radius[None, :], currents], 0)
    ordered = jnp.zeros_like(packed).at[:, slot_of].set(packed)
    row_block = lax.all_gather(ordered, "col", axis=1, tiled=True)
    col_block = lax.all_gather(ordered, "row", axis=1, tiled=True)
    col_count = lax.axis_size("col")
    row_count = lax.axis_size("row")
    row_pos = lax.axis_index("row")
    per_device = local_count // CS
    row_span = per_device * col_count
    col_span = per_device * row_count
    slot_count = pair_list.shape[0]
    local_first = pair_list[:, 0] - row_pos * row_span
    local_second = pair_list[:, 1] // row_span * per_device + pair_list[:, 1] % per_device
    diagonal_all = (pair_list[:, 0] == pair_list[:, 1]).astype(jnp.int32)

    def add_terms(sums_pair, slot_index, direct_part, mirror_part):
        row_sum, col_sum = sums_pair
        first_id = local_first[slot_index]
        second_id = local_second[slot_index]
        current = lax.dynamic_slice_in_dim(row_sum, first_id * CS, CS, 1)
        row_sum = lax.dynamic_update_slice_in_dim(row_sum, current + direct_part, first_id * CS, 1)
        current = lax.dynamic_slice_in_dim(col_sum, second_id * CS, CS, 1)
        col_sum = lax.dynamic_update_slice_in_dim(col_sum, current + mirror_part, second_id * CS, 1)
        return (row_sum, col_sum)

    row_start = jnp.zeros((2, row_span * CS), jnp.float32)
    col_start = jnp.zeros((2, col_span * CS), jnp.float32)
    half_count = slot_count // 2

    def visit_group(group_index, sums_now):
        for inner in range(group_size):
            slot_index = group_index * group_size + inner
            block_first = lax.dynamic_slice_in_dim(row_block, local_first[slot_index] * CS, CS, 1)
            block_second = lax.dynamic_slice_in_dim(col_block, local_second[slot_index] * CS, CS, 1)
            direct_part, mirror_part = slot_terms(
                block_first, block_second, near_flag[slot_index], diagonal_all[slot_index] > 0
            )
            sums_now = add_terms(sums_now, slot_index, direct_part, mirror_part)
        return sums_now

    row_sum, col_sum = lax.fori_loop(
        0, half_count // group_size, visit_group, (row_start, col_start)
    )
    row_tiles = row_block.reshape(9, row_span, CS)
    col_tiles = col_block.reshape(9, col_span, CS)
    lent_first = jnp.take(row_tiles, local_first[half_count:], axis=1)
    lent_second = jnp.take(col_tiles, local_second[half_count:], axis=1)
    lent_blocks = jnp.concatenate([lent_first, lent_second], 0)
    lent_codes = (near_flag[half_count:] + 3 * diagonal_all[half_count:]).astype(jnp.float32)
    top_bit = lax.axis_size("row").bit_length() - 2
    borrowed_blocks, borrowed_codes = partner((lent_blocks, lent_codes), "row", top_bit)

    def help_group(group_index, results):
        for inner in range(group_size):
            item = group_index * group_size + inner
            block_pair = lax.dynamic_index_in_dim(borrowed_blocks, item, 1, keepdims=False)
            code_value = borrowed_codes[item].astype(jnp.int32)
            direct_part, mirror_part = slot_terms(
                block_pair[0:9], block_pair[9:18], code_value % 3, code_value // 3 > 0
            )
            both_parts = jnp.stack([direct_part, mirror_part])[:, :, None, :]
            results = lax.dynamic_update_slice(results, both_parts, (0, 0, item, 0))
        return results

    helped = lax.fori_loop(
        0, half_count // group_size, help_group, jnp.zeros((2, 2, half_count, CS), jnp.float32)
    )
    returned = partner(helped, "row", top_bit)
    row_sum = (
        row_sum.reshape(2, row_span, CS)
        .at[:, local_first[half_count:], :]
        .add(returned[0])
        .reshape(2, row_span * CS)
    )
    col_sum = (
        col_sum.reshape(2, col_span, CS)
        .at[:, local_second[half_count:], :]
        .add(returned[1])
        .reshape(2, col_span * CS)
    )
    owned = lax.psum_scatter(row_sum, "col", scatter_dimension=1, tiled=True) + lax.psum_scatter(
        col_sum, "row", scatter_dimension=1, tiled=True
    )
    induced = owned[:, slot_of]
    voltage_real = resist * currents[0] - induced[1]
    voltage_imag = resist * currents[1] + induced[0]
    return jnp.stack([voltage_real, voltage_imag])


def solution(mesh):
    return jax.shard_map(
        on_device,
        mesh=mesh,
        in_specs=(
            P(None, ("row", "col")),
            P(None, ("row", "col")),
            P(("row", "col")),
            P(None, ("row", "col")),
            P(("row", "col")),
            P(("row", "col")),
            P(("row", "col"), None),
            P(("row", "col")),
        ),
        out_specs=P(None, ("row", "col")),
        check_vma=False,
    )
```

profile of v0, /device:TPU:0, one launch (start us, length us, event | category | flops | bytes accessed | tf_op | source)
XLA Modules:
  0.0 471.0 jit_solution(10847752534651488676)
XLA Ops:
  6.5 0.7 broadcast_clamp_fusion
  7.2 0.8 maximum_bitcast_fusion.8
  8.3 3.2 scatter_custom_fusion
  11.5 39.7 %all_gather.7 = f32[9,4096]{0,1:T(8,128)S(1)} all-gather(f32[9,1024]{0,1:T(8,128)S(1)} %scatter_custom_fusion), channel_id=1, replica_groups=mesh['row'=8,'col'=4] {'col'}, dimensions={1}, use_global_device_ids=true | all-gather | bytes 184320 | tf_op jit(solution)/shard_map/all_gather | solution.py:104
  51.2 24.6 %all_gather.6 = f32[9,8192]{0,1:T(8,128)} all-gather(f32[9,1024]{0,1:T(8,128)S(1)} %scatter_custom_fusion), channel_id=1, replica_groups=mesh['row'=8,'col'=4] {'row'}, dimensions={1}, use_global_device_ids=true | all-gather | bytes 331776 | tf_op jit(solution)/shard_map/all_gather | solution.py:105
  76.6 2.9 copy.23
  80.0 1.4 gather_fusion.1
  81.5 1.2 select_bitcast_fusion
  83.3 2.0 collective-permute-start
  85.9 2.9 copy.20
  88.8 10.1 %collective-permute-done.1 = f32[18,16,512]{2,1,0:T(8,128)} collective-permute-done((f32[18,16,512]{2,1,0:T(8,128)S(1)}, f32[18,16,512]{2,1,0:T(8,128)}, u32[]{:S(2)}, u32[]{:S(2)}) %collective-permute-start.1) | collective-permute-done | bytes 589856 | tf_op jit(solution)/shard_map/ppermute | solution.py:23
  98.9 1.4 copy.25
  100.4 49.9 %while.34 = (s32[]{:T(128)}, f32[2,2,16,512]{3,1,0,2:T(2,128)S(1)}, f32[16]{0:T(128)S(1)}, f32[18,16,512]{2,0,1:T(8,128)S(1)}, s32[]{:T(128)}, /*index=5*/s32[]{...) while((s32[]{:T(128)}, f32[2,2,16,512]{3,1,0,2:T(2,128)S(1)}, ...), condition=%wide.region_84.85_spmd, body=%wide.region_43.84_spmd.sunk | while | flops 108167224 | bytes 22711308 | solution.py:166
  104.0 4.4 conditional.55
  108.4 4.5 conditional.54
  112.9 4.5 conditional.53
  120.9 5.8 %conditional.55 = (f32[1,2,512]{2,1,0:T(2,128)S(1)}, f32[1,2,512]{2,1,0:T(2,128)S(1)}) conditional(s32[]{:T(128)} %convert_element_type.273, () %tuple.1100, (f32[18,16,512]{2,0,1:T(8,128)S(1)}, s32[]{:T(128)}, s32[]{:T(128)}, s32[]{:T(128)}) %tuple.1101), branch_computations={%region_74.74_spmd, %region_75.83_spmd} | conditional | flops 27039752 | bytes 5661238 | solution.py:97
  126.8 4.5 conditional.52
  134.7 5.8 %conditional.55 = (f32[1,2,512]{2,1,0:T(2,128)S(1)}, f32[1,2,512]{2,1,0:T(2,128)S(1)}) conditional(s32[]{:T(128)} %convert_element_type.273, () %tuple.1100, (f32[18,16,512]{2,0,1:T(8,128)S(1)}, s32[]{:T(128)}, s32[]{:T(128)}, s32[]{:T(128)}) %tuple.1101), branch_computations={%region_74.74_spmd, %region_75.83_spmd} | conditional | flops 27039752 | bytes 5661238 | solution.py:97
  140.6 5.8 %conditional.52 = (f32[1,2,512]{2,1,0:T(2,128)S(1)}, f32[1,2,512]{2,1,0:T(2,128)S(1)}) conditional(s32[]{:T(128)} %convert_element_type.267, () %tuple.1094, (f32[18,16,512]{2,0,1:T(8,128)S(1)}, s32[]{:T(128)}, s32[]{:T(128)}, s32[]{:T(128)}) %tuple.1095), branch_computations={%region_44.44_spmd, %region_45.53_spmd} | conditional | flops 27039752 | bytes 5661238 | solution.py:97
  150.2 40.1 %collective-permute-start.2 = (f32[2,2,16,512]{3,1,0,2:T(2,128)S(1)}, f32[2,2,16,512]{3,1,0,2:T(2,128)S(1)}, u32[]{:S(2)}, u32[]{:S(2)}) collective-permute-start(f32[2,2,16,512]{3,1,0,2:T(2,128)S(1)} %get-tuple-element.1886), channel_id=1, source_target_pairs={{0,16},{16,0},{4,20},{20,4},{8,24},{24,8},{12,28},{28,12},{1,17},{... | collective-permute-start | bytes 393224 | tf_op jit(solution)/shard_map/ppermute | solution.py:23
  190.4 171.7 %while.33 = (s32[]{:T(128)}, f32[2,4096]{1,0:T(2,128)S(1)}, f32[2,8192]{1,0:T(2,128)S(1)}, s32[32]{0:T(128)S(1)}, s32[32]{0:T(128)S(1)}, /*index=5*/s32[32]{0:T(...) while((s32[]{:T(128)}, f32[2,4096]{1,0:T(2,128)S(1)}, ...), condition=%wide.region_42.43_spmd, body=%wide.region_1.42_spmd.sunk | while | flops 108167248 | bytes 22744584 | solution.py:142
  207.7 0.7 fusion.709
  214.1 8.1 %conditional.51 = (f32[2,512]{1,0:T(2,128)S(1)}, f32[2,512]{1,0:T(2,128)S(1)}) conditional(s32[]{:T(128)} %convert_element_type.265, () %tuple.1090, (f32[9,8192]{1,0:T(8,128)S(1)}, s32[]{:T(128)}, f32[9,4096]{1,0:T(8,128)S(1)}, s32[]{:T(128)}, s32[]{:T(128)}, /*index=5*/s32[32]{0:T(128)S(1)}, s32[]{:T(128)}) %tuple.1091), branch_computations={%region_32.32_spmd, %region_33.41_spmd} | conditional | flops 27039756 | bytes 5661272 | solution.py:97
  222.2 8.2 %conditional.50 = (f32[2,512]{1,0:T(2,128)S(1)}, f32[2,512]{1,0:T(2,128)S(1)}) conditional(s32[]{:T(128)} %convert_element_type.264, () %tuple.1088, (f32[9,8192]{1,0:T(8,128)S(1)}, s32[]{:T(128)}, f32[9,4096]{1,0:T(8,128)S(1)}, s32[]{:T(128)}, s32[]{:T(128)}, /*index=5*/s32[32]{0:T(128)S(1)}, s32[]{:T(128)}) %tuple.1089), branch_computations={%region_22.22_spmd, %region_23.31_spmd} | conditional | flops 27039756 | bytes 5661272 | solution.py:97
  230.4 6.8 %conditional.49 = (f32[2,512]{1,0:T(2,128)S(1)}, f32[2,512]{1,0:T(2,128)S(1)}) conditional(s32[]{:T(128)} %convert_element_type.263, () %tuple.1086, (f32[9,8192]{1,0:T(8,128)S(1)}, s32[]{:T(128)}, f32[9,4096]{1,0:T(8,128)S(1)}, s32[]{:T(128)}, s32[]{:T(128)}, /*index=5*/s32[32]{0:T(128)S(1)}, s32[]{:T(128)}) %tuple.1087), branch_computations={%region_12.12_spmd, %region_13.21_spmd} | conditional | flops 27039756 | bytes 5661272 | solution.py:97
  237.2 8.2 %conditional.48 = (f32[2,512]{1,0:T(2,128)S(1)}, f32[2,512]{1,0:T(2,128)S(1)}) conditional(s32[]{:T(128)} %convert_element_type.262, () %tuple.1084, (f32[9,8192]{1,0:T(8,128)S(1)}, s32[]{:T(128)}, f32[9,4096]{1,0:T(8,128)S(1)}, s32[]{:T(128)}, s32[]{:T(128)}, /*index=5*/s32[32]{0:T(128)S(1)}, s32[]{:T(128)}) %tuple.1085), branch_computations={%region_2.2_spmd, %region_3.11_spmd} | conditional | flops 27039756 | bytes 5661272 | solution.py:97
  248.8 0.7 fusion.709
  255.2 8.1 %conditional.51 = (f32[2,512]{1,0:T(2,128)S(1)}, f32[2,512]{1,0:T(2,128)S(1)}) conditional(s32[]{:T(128)} %convert_element_type.265, () %tuple.1090, (f32[9,8192]{1,0:T(8,128)S(1)}, s32[]{:T(128)}, f32[9,4096]{1,0:T(8,128)S(1)}, s32[]{:T(128)}, s32[]{:T(128)}, /*index=5*/s32[32]{0:T(128)S(1)}, s32[]{:T(128)}) %tuple.1091), branch_computations={%region_32.32_spmd, %region_33.41_spmd} | conditional | flops 27039756 | bytes 5661272 | solution.py:97
  263.3 8.2 %conditional.50 = (f32[2,512]{1,0:T(2,128)S(1)}, f32[2,512]{1,0:T(2,128)S(1)}) conditional(s32[]{:T(128)} %convert_element_type.264, () %tuple.1088, (f32[9,8192]{1,0:T(8,128)S(1)}, s32[]{:T(128)}, f32[9,4096]{1,0:T(8,128)S(1)}, s32[]{:T(128)}, s32[]{:T(128)}, /*index=5*/s32[32]{0:T(128)S(1)}, s32[]{:T(128)}) %tuple.1089), branch_computations={%region_22.22_spmd, %region_23.31_spmd} | conditional | flops 27039756 | bytes 5661272 | solution.py:97
  271.5 8.2 %conditional.49 = (f32[2,512]{1,0:T(2,128)S(1)}, f32[2,512]{1,0:T(2,128)S(1)}) conditional(s32[]{:T(128)} %convert_element_type.263, () %tuple.1086, (f32[9,8192]{1,0:T(8,128)S(1)}, s32[]{:T(128)}, f32[9,4096]{1,0:T(8,128)S(1)}, s32[]{:T(128)}, s32[]{:T(128)}, /*index=5*/s32[32]{0:T(128)S(1)}, s32[]{:T(128)}) %tuple.1087), branch_computations={%region_12.12_spmd, %region_13.21_spmd} | conditional | flops 27039756 | bytes 5661272 | solution.py:97
  279.7 6.8 %conditional.48 = (f32[2,512]{1,0:T(2,128)S(1)}, f32[2,512]{1,0:T(2,128)S(1)}) conditional(s32[]{:T(128)} %convert_element_type.262, () %tuple.1084, (f32[9,8192]{1,0:T(8,128)S(1)}, s32[]{:T(128)}, f32[9,4096]{1,0:T(8,128)S(1)}, s32[]{:T(128)}, s32[]{:T(128)}, /*index=5*/s32[32]{0:T(128)S(1)}, s32[]{:T(128)}) %tuple.1085), branch_computations={%region_2.2_spmd, %region_3.11_spmd} | conditional | flops 27039756 | bytes 5661272 | solution.py:97
  296.2 6.7 %conditional.51 = (f32[2,512]{1,0:T(2,128)S(1)}, f32[2,512]{1,0:T(2,128)S(1)}) conditional(s32[]{:T(128)} %convert_element_type.265, () %tuple.1090, (f32[9,8192]{1,0:T(8,128)S(1)}, s32[]{:T(128)}, f32[9,4096]{1,0:T(8,128)S(1)}, s32[]{:T(128)}, s32[]{:T(128)}, /*index=5*/s32[32]{0:T(128)S(1)}, s32[]{:T(128)}) %tuple.1091), branch_computations={%region_32.32_spmd, %region_33.41_spmd} | conditional | flops 27039756 | bytes 5661272 | solution.py:97
  303.0 6.8 %conditional.50 = (f32[2,512]{1,0:T(2,128)S(1)}, f32[2,512]{1,0:T(2,128)S(1)}) conditional(s32[]{:T(128)} %convert_element_type.264, () %tuple.1088, (f32[9,8192]{1,0:T(8,128)S(1)}, s32[]{:T(128)}, f32[9,4096]{1,0:T(8,128)S(1)}, s32[]{:T(128)}, s32[]{:T(128)}, /*index=5*/s32[32]{0:T(128)S(1)}, s32[]{:T(128)}) %tuple.1089), branch_computations={%region_22.22_spmd, %region_23.31_spmd} | conditional | flops 27039756 | bytes 5661272 | solution.py:97
  309.8 6.8 %conditional.49 = (f32[2,512]{1,0:T(2,128)S(1)}, f32[2,512]{1,0:T(2,128)S(1)}) conditional(s32[]{:T(128)} %convert_element_type.263, () %tuple.1086, (f32[9,8192]{1,0:T(8,128)S(1)}, s32[]{:T(128)}, f32[9,4096]{1,0:T(8,128)S(1)}, s32[]{:T(128)}, s32[]{:T(128)}, /*index=5*/s32[32]{0:T(128)S(1)}, s32[]{:T(128)}) %tuple.1087), branch_computations={%region_12.12_spmd, %region_13.21_spmd} | conditional | flops 27039756 | bytes 5661272 | solution.py:97
  316.6 6.8 %conditional.48 = (f32[2,512]{1,0:T(2,128)S(1)}, f32[2,512]{1,0:T(2,128)S(1)}) conditional(s32[]{:T(128)} %convert_element_type.262, () %tuple.1084, (f32[9,8192]{1,0:T(8,128)S(1)}, s32[]{:T(128)}, f32[9,4096]{1,0:T(8,128)S(1)}, s32[]{:T(128)}, s32[]{:T(128)}, /*index=5*/s32[32]{0:T(128)S(1)}, s32[]{:T(128)}) %tuple.1085), branch_computations={%region_2.2_spmd, %region_3.11_spmd} | conditional | flops 27039756 | bytes 5661272 | solution.py:97
  333.1 6.7 %conditional.51 = (f32[2,512]{1,0:T(2,128)S(1)}, f32[2,512]{1,0:T(2,128)S(1)}) conditional(s32[]{:T(128)} %convert_element_type.265, () %tuple.1090, (f32[9,8192]{1,0:T(8,128)S(1)}, s32[]{:T(128)}, f32[9,4096]{1,0:T(8,128)S(1)}, s32[]{:T(128)}, s32[]{:T(128)}, /*index=5*/s32[32]{0:T(128)S(1)}, s32[]{:T(128)}) %tuple.1091), branch_computations={%region_32.32_spmd, %region_33.41_spmd} | conditional | flops 27039756 | bytes 5661272 | solution.py:97
  339.9 6.8 %conditional.50 = (f32[2,512]{1,0:T(2,128)S(1)}, f32[2,512]{1,0:T(2,128)S(1)}) conditional(s32[]{:T(128)} %convert_element_type.264, () %tuple.1088, (f32[9,8192]{1,0:T(8,128)S(1)}, s32[]{:T(128)}, f32[9,4096]{1,0:T(8,128)S(1)}, s32[]{:T(128)}, s32[]{:T(128)}, /*index=5*/s32[32]{0:T(128)S(1)}, s32[]{:T(128)}) %tuple.1089), branch_computations={%region_22.22_spmd, %region_23.31_spmd} | conditional | flops 27039756 | bytes 5661272 | solution.py:97
  346.7 8.2 %conditional.49 = (f32[2,512]{1,0:T(2,128)S(1)}, f32[2,512]{1,0:T(2,128)S(1)}) conditional(s32[]{:T(128)} %convert_element_type.263, () %tuple.1086, (f32[9,8192]{1,0:T(8,128)S(1)}, s32[]{:T(128)}, f32[9,4096]{1,0:T(8,128)S(1)}, s32[]{:T(128)}, s32[]{:T(128)}, /*index=5*/s32[32]{0:T(128)S(1)}, s32[]{:T(128)}) %tuple.1087), branch_computations={%region_12.12_spmd, %region_13.21_spmd} | conditional | flops 27039756 | bytes 5661272 | solution.py:97
  354.9 6.8 %conditional.48 = (f32[2,512]{1,0:T(2,128)S(1)}, f32[2,512]{1,0:T(2,128)S(1)}) conditional(s32[]{:T(128)} %convert_element_type.262, () %tuple.1084, (f32[9,8192]{1,0:T(8,128)S(1)}, s32[]{:T(128)}, f32[9,4096]{1,0:T(8,128)S(1)}, s32[]{:T(128)}, s32[]{:T(128)}, /*index=5*/s32[32]{0:T(128)S(1)}, s32[]{:T(128)}) %tuple.1085), branch_computations={%region_2.2_spmd, %region_3.11_spmd} | conditional | flops 27039756 | bytes 5661272 | solution.py:97
  362.1 1.2 scatter_fusion
  363.3 2.0 copy.26
  365.4 1.2 scatter_fusion.1
  366.6 2.7 copy.27
  369.4 35.6 %reduce-scatter.3.cloned.1.call-done = f32[2,1024]{0,1:T(8,128)} async-done(((f32[2,4096]{0,1:T(8,128)}), f32[2,1024]{0,1:T(8,128)}) %reduce-scatter.3.cloned.1.call-update) | async-done | bytes 8208 | tf_op jit(solution)/shard_map/reduce_scatter | solution.py:182
  405.0 53.8 %reduce-scatter.5.cloned.1.call-done = f32[2,1024]{0,1:T(8,128)} async-done(((f32[2,8192]{0,1:T(8,128)}), f32[2,1024]{0,1:T(8,128)}) %reduce-scatter.5.cloned.1.call-update) | async-done | bytes 8208 | tf_op jit(solution)/shard_map/reduce_scatter | solution.py:182
  458.8 1.3 add.6301
  460.0 2.8 gather_fusion.2
  (850 shorter events, 174.5 us)
Async XLA Ops:
  6.5 398.5 %reduce-scatter.3.cloned.1.call-start = ((), (), s32[]{:S(2)}) async-start(), calls=%async_computation.2 | async-start | bytes 2621440 | tf_op jit(solution)/shard_map/reduce_scatter | solution.py:182
  8.0 67.7 %copy-start.3 = (s32[32,2]{0,1:T(2,128)S(1)}, s32[32,2]{0,1:T(2,128)}, u32[]{:S(2)}) copy-start(s32[32,2]{0,1:T(2,128)} %param.98) | copy-start | bytes 772
  79.4 3.8 copy-start
  83.1 15.8 %collective-permute-start.1 = (f32[18,16,512]{2,1,0:T(8,128)S(1)}, f32[18,16,512]{2,1,0:T(8,128)}, u32[]{:S(2)}, u32[]{:S(2)}) collective-permute-start(f32[18,16,512]{2,1,0:T(8,128)S(1)} %copy.24), channel_id=1, source_target_pairs={{0,16},{16,0},{4,20},{20,4},{8,24},{24,8},{12,28},{28,12},{1,17},{... | collective-permute-start | bytes 1769480 | tf_op jit(solution)/shard_map/ppermute | solution.py:23
  83.3 17.0 %collective-permute-start = (f32[16]{0:T(128)S(1)}, f32[16]{0:T(128)S(1)}, u32[]{:S(2)}, u32[]{:S(2)}) collective-permute-start(f32[16]{0:T(128)S(1)} %add_convert_fusion), channel_id=1, source_target_pairs={{0,16},{16,0},{4,20},{20,4},{8,24},{24,8},{12,28},{28,12},{1,17},{... | collective-permute-start | bytes 200 | tf_op jit(solution)/shard_map/ppermute | solution.py:23
  150.2 211.8 %collective-permute-start.2 = (f32[2,2,16,512]{3,1,0,2:T(2,128)S(1)}, f32[2,2,16,512]{3,1,0,2:T(2,128)S(1)}, u32[]{:S(2)}, u32[]{:S(2)}) collective-permute-start(f32[2,2,16,512]{3,1,0,2:T(2,128)S(1)} %get-tuple-element.1886), channel_id=1, source_target_pairs={{0,16},{16,0},{4,20},{20,4},{8,24},{24,8},{12,28},{28,12},{1,17},{... | collective-permute-start | bytes 393224 | tf_op jit(solution)/shard_map/ppermute | solution.py:23
  365.3 93.4 %reduce-scatter.5.cloned.1.call-start = ((), (), s32[]{:S(2)}) async-start(), calls=%async_computation.3 | async-start | bytes 4718592 | tf_op jit(solution)/shard_map/reduce_scatter | solution.py:182
  366.6 2.8 copy-start.1
  369.3 94.0 %copy-start.2 = (f32[1024]{0:T(1024)S(1)}, f32[1024]{0:T(1024)}, u32[]{:S(2)}) copy-start(f32[1024]{0:T(1024)} %param.96) | copy-start | bytes 12292
Sparse Core Ops, SparseCore 0:
  365.5 39.4 reduce-scatter.2
  408.3 50.3 reduce-scatter.4
where the time goes:
time: 480 us; the launch traced here: 471 us
  waiting for transfers between devices  99.6 us (21%)
  loops' own time  83.7 us (17%)
  matrix products  74.7 us (16%)
  blocking collectives  64.3 us (13%)
  local copies, waits for them, and re-layouts  48.1 us (10%)
  other arithmetic  44.7 us (9%)
  starting transfers between devices  42.2 us (9%)
  between operations  13.9 us (3%)
    reduce_scatter x1, waiting for transfers between devices, on_device(): lax.psum_scatter(col_sum, 'row', scatter_dimension=1, tiled=True)  53.8 us
    another operation x1, loops' own time, on_device(): lax.fori_loop(0, half_count // group_size, visit_group, (row_start, col_s...  45 us
    ppermute x3, starting transfers between devices, partner(): return lax.ppermute(block, axis, route)  42.2 us
    all_gather x1, blocking collectives, on_device(): row_block = lax.all_gather(ordered, 'col', axis=1, tiled=True)  39.7 us
    dot_general x92, matrix products, live_terms(): jnp.dot(block_second[7:9], kernel_tile.T, precision=lax.Precision.HIGHEST)  39.3 us
    reduce_scatter x1, waiting for transfers between devices, on_device(): lax.psum_scatter(row_sum, 'col', scatter_dimension=1, tiled=True)  35.6 us
    dot_general x92, matrix products, live_terms(): jnp.dot(portion[7:9], kernel_tile, precision=lax.Precision.HIGHEST)  35.4 us
    all_gather x1, blocking collectives, on_device(): col_block = lax.all_gather(ordered, 'row', axis=1, tiled=True)  24.6 us
  transfers between devices with their start and end apart: 5, of which 3 were waited for; matrix products, arithmetic and copies ran while one was open for 23% of the time, Pallas kernels for 0%

commit v1 on v0

v1 whole, which is shorter than its diff:
```python
import functools
import math

import jax
import jax.numpy as jnp
from jax import lax
from jax.experimental import pallas as pl
from jax.experimental.pallas import tpu as pltpu
from jax.sharding import PartitionSpec as P

CS = 512
F32 = jnp.float32
BF16 = jnp.bfloat16
MESH = pl.DeviceIdType.MESH
gauss_step = 0.5 / math.sqrt(3.0)
kernel_gain = 0.25
VMEM = pl.BlockSpec(memory_space=pltpu.VMEM)
CHUNK = 256


def split_three(value):
    high = value.astype(BF16).astype(F32)
    rest = value - high
    middle = rest.astype(BF16).astype(F32)
    return high, middle, rest - middle


def dot_nn(left, right):
    return lax.dot_general(left, right, (((1,), (0,)), ((), ())), preferred_element_type=F32)


def dot_nt(left, right):
    return lax.dot_general(left, right, (((1,), (1,)), ((), ())), preferred_element_type=F32)


def one_hot_rows(slots, start, count):
    rows = lax.broadcasted_iota(jnp.int32, (count, slots.shape[1]), 0) + start
    return jnp.where(rows == slots, 1.0, 0.0).astype(BF16)


def order_kernel(pos, seg, rad, cur, slot, pair, flag, main, extra, stack):
    clusters = main.shape[0]
    slots = slot[...]
    stack[...] = jnp.zeros_like(stack)
    for source, row in ((pos, 0), (seg, 3), (rad, 6), (cur, 7)):
        count = source.shape[0]
        for part, piece in enumerate(split_three(source[...])):
            stack[part * 16 + row : part * 16 + row + count, :] = piece
    parts = stack[...].astype(BF16)
    for cluster in range(clusters):
        sums = dot_nt(parts, one_hot_rows(slots, cluster * CS, CS))
        ordered = sums[0:16] + sums[16:32] + sums[32:48]
        main[cluster] = ordered[0:8]
        extra[cluster : cluster + 1, :] = ordered[8:9]
    listed = pair.shape[1]
    extra[clusters : clusters + 2, :] = jnp.zeros((2, CS), F32)
    extra[clusters : clusters + 1, 0:listed] = pair[0:1, :].astype(F32)
    extra[clusters : clusters + 1, 128 : 128 + listed] = pair[1:2, :].astype(F32)
    extra[clusters : clusters + 1, 256 : 256 + listed] = flag[...].astype(F32)


def order_elements(positions, segments, radius, currents, slot_of, pair_list, near_flag):
    local = positions.shape[1]
    clusters = local // CS
    return pl.pallas_call(
        order_kernel,
        out_shape=(
            jax.ShapeDtypeStruct((clusters, 8, CS), F32),
            jax.ShapeDtypeStruct((clusters + 2, CS), F32),
        ),
        in_specs=[VMEM] * 7,
        out_specs=(VMEM, VMEM),
        scratch_shapes=[pltpu.VMEM((48, local), F32)],
    )(
        positions,
        segments,
        radius[None, :],
        currents,
        slot_of[None, :],
        pair_list.T,
        near_flag[None, :],
    )


def pair_kernel(main, extra, total, feat_first, feat_second, weight_first, weight_second):
    devices, clusters = main.shape[0], main.shape[1]
    me = lax.axis_index("row") * lax.axis_size("col") + lax.axis_index("col")
    total[...] = jnp.zeros_like(total)
    for feat, ones in ((feat_first, 21), (feat_second, 18)):
        feat[...] = jnp.zeros_like(feat)
        for sign in range(2):
            feat[sign, ones : ones + 3, :] = jnp.ones((3, CS), F32)
    weight_first[...] = jnp.zeros_like(weight_first)
    weight_second[...] = jnp.zeros_like(weight_second)

    lists = extra[:, clusters, :]
    first_ids, second_ids, flags = lists[:, 0:128], lists[:, 128:256], lists[:, 256:384]
    code = (first_ids * 1024.0 + second_ids) * 4.0 + flags
    is_near = jnp.where(flags > 1.5, 1.0, 0.0)
    is_far = jnp.where(jnp.abs(flags - 1.0) < 0.5, 1.0, 0.0)
    before_lane = jnp.where(
        lax.broadcasted_iota(jnp.int32, (128, 128), 0) < lax.broadcasted_iota(jnp.int32, (128, 128), 1),
        1.0,
        0.0,
    ).astype(BF16)
    before_row = jnp.where(
        lax.broadcasted_iota(jnp.int32, (devices, devices), 1)
        < lax.broadcasted_iota(jnp.int32, (devices, devices), 0),
        1.0,
        0.0,
    ).astype(BF16)

    def rank_in(mask):
        in_row = dot_nn(mask.astype(BF16), before_lane)
        above = jnp.sum(dot_nn(before_row, mask.astype(BF16)), axis=1, keepdims=True)
        return in_row + above

    near_count = jnp.sum(is_near)
    live_count = near_count + jnp.sum(is_far)
    rank = jnp.where(
        is_near > 0.5,
        rank_in(is_near),
        jnp.where(is_far > 0.5, rank_in(is_far) + near_count, -1.0),
    ).astype(jnp.int32)
    mine = (live_count.astype(jnp.int32) + (devices - 1 - me)) // devices

    def pick(turn):
        found = jnp.where(rank == turn * devices + me, code, 0.0)
        return jnp.sum(found).astype(jnp.int32)

    def load(cluster, weights):
        device, local = cluster // clusters, cluster % clusters
        block = main[device, local]
        imag = extra[device, pl.ds(local, 1), :]
        wide = []
        for axis in range(3):
            vector = block[3 + axis : 4 + axis]
            for part, current in enumerate((block[7:8], imag)):
                product = vector * current
                high = product.astype(BF16).astype(F32)
                row = 2 * axis + part
                weights[row : row + 1, :] = high
                weights[8 + row : 9 + row, :] = product - high
        return block

    def write_first(sign, points, radii):
        norm = jnp.sum(points * points, axis=0, keepdims=True) + radii * radii
        high, middle, low = split_three(points)
        for slot, piece in enumerate((high, high, middle, middle, high, low)):
            feat_first[sign, 3 * slot : 3 * slot + 3, :] = piece
        for row, piece in enumerate(split_three(norm)):
            feat_first[sign, 18 + row : 19 + row, :] = piece

    def write_second(sign, points, radii):
        norm = jnp.sum(points * points, axis=0, keepdims=True) + radii * radii
        high, middle, low = split_three(-2.0 * points)
        for slot, piece in enumerate((high, middle, high, middle, low, high)):
            feat_second[sign, 3 * slot : 3 * slot + 3, :] = piece
        for row, piece in enumerate(split_three(norm)):
            feat_second[sign, 21 + row : 22 + row, :] = piece

    def contract(sums, block, scale):
        both = sums[0:8] + sums[8:16]
        result = 0.0
        for axis in range(3):
            result = result + both[2 * axis : 2 * axis + 2] * block[3 + axis : 4 + axis]
        return result * scale

    def apply(signs, first, second, block_first, block_second, scale):
        for sign in range(signs):
            step = (gauss_step if sign else -gauss_step) if signs > 1 else 0.0
            for block, write in ((block_first, write_first), (block_second, write_second)):
                points = block[0:3] - 0.5
                if signs > 1:
                    points = points + step * block[3:6]
                write(sign, points, block[6:7])
        left = [feat_first[sign].T.astype(BF16) for sign in range(signs)]
        right = [feat_second[sign].astype(BF16) for sign in range(signs)]
        from_first = weight_first[...].astype(BF16)
        from_second = weight_second[...].astype(BF16)
        mirror = jnp.zeros((16, CS), F32)
        direct = []
        for start in range(0, CS, CHUNK):
            inverse = 0.0
            for one in left:
                for other in right:
                    inverse = inverse + lax.rsqrt(dot_nn(one[start : start + CHUNK], other))
            high = inverse.astype(BF16)
            low = (inverse - high.astype(F32)).astype(BF16)
            direct.append(dot_nt(from_second, high) + dot_nt(from_second, low))
            rows = from_first[:, start : start + CHUNK]
            mirror = mirror + dot_nn(rows, high) + dot_nn(rows, low)
        direct = jnp.concatenate(direct, 1)
        total[first] += contract(direct, block_first, scale)
        keep = jnp.where(first == second, 0.0, scale)
        total[second] += contract(mirror, block_second, keep)

    def visit(turn, now):
        flag = now % 4
        second = now // 4 % 1024
        first = now // 4096
        block_first = load(first, weight_first)
        block_second = load(second, weight_second)

        @pl.when(flag == 2)
        def _():
            apply(2, first, second, block_first, block_second, kernel_gain * 0.25)

        @pl.when(flag != 2)
        def _():
            apply(1, first, second, block_first, block_second, kernel_gain)

        return pick(turn + 1)

    lax.fori_loop(0, mine, visit, pick(0))


def pair_terms(main, extra):
    devices, clusters = main.shape[0], main.shape[1]
    return pl.pallas_call(
        pair_kernel,
        out_shape=jax.ShapeDtypeStruct((devices * clusters, 2, CS), F32),
        in_specs=[VMEM, VMEM],
        out_specs=VMEM,
        scratch_shapes=[
            pltpu.VMEM((2, 32, CS), F32),
            pltpu.VMEM((2, 32, CS), F32),
            pltpu.VMEM((16, CS), F32),
            pltpu.VMEM((16, CS), F32),
        ],
    )(main, extra)


def finish_kernel(owned, resist, cur, slot, out, stack):
    clusters = owned.shape[0]
    slots = slot[...]
    sums = jnp.zeros((16, slots.shape[1]), F32)
    stack[...] = jnp.zeros_like(stack)
    for cluster in range(clusters):
        for part, piece in enumerate(split_three(owned[cluster])):
            stack[2 * part : 2 * part + 2, :] = piece
        sums = sums + dot_nn(stack[...].astype(BF16), one_hot_rows(slots, cluster * CS, CS))
    induced = sums[0:2] + sums[2:4] + sums[4:6]
    scaled = resist[...] * cur[...]
    out[0:1, :] = scaled[0:1] - induced[1:2]
    out[1:2, :] = scaled[1:2] + induced[0:1]


def finish(owned, resist, currents, slot_of):
    return pl.pallas_call(
        finish_kernel,
        out_shape=jax.ShapeDtypeStruct(currents.shape, F32),
        in_specs=[VMEM] * 4,
        out_specs=VMEM,
        scratch_shapes=[pltpu.VMEM((16, CS), F32)],
    )(owned, resist[None, :], currents, slot_of[None, :])


def on_device(positions, segments, radius, currents, resist, slot_of, pair_list, near_flag):
    main, extra = order_elements(
        positions, segments, radius, currents, slot_of, pair_list, near_flag
    )
    main_all = lax.all_gather(main, ("row", "col"))
    extra_all = lax.all_gather(extra, ("row", "col"))
    total = pair_terms(main_all, extra_all)
    owned = lax.psum_scatter(total, ("row", "col"), scatter_dimension=0, tiled=True)
    return finish(owned, resist, currents, slot_of)


def solution(mesh):
    return jax.shard_map(
        on_device,
        mesh=mesh,
        in_specs=(
            P(None, ("row", "col")),
            P(None, ("row", "col")),
            P(("row", "col")),
            P(None, ("row", "col")),
            P(("row", "col")),
            P(("row", "col")),
            P(("row", "col"), None),
            P(("row", "col")),
        ),
        out_specs=P(None, ("row", "col")),
        check_vma=False,
    )
```

time: 480 us -> 241 us (0.50); the launches traced: 471 us -> 240 us
  loops' own time: 83.7 us -> 0 us
  matrix products: 74.7 us -> 0 us
  local copies, waits for them, and re-layouts: 48.1 us -> 1.91 us
  other arithmetic: 44.7 us -> 0 us
  starting transfers between devices: 42.2 us -> 0.04 us
  Pallas kernels: 0 us -> 25.3 us
  waiting for transfers between devices: 99.6 us -> 123 us
  blocking collectives: 64.3 us -> 76.7 us
    unnamed x2 -> x3, waiting for transfers between devices: 0.03 us -> 123 us
    reduce_scatter x2 -> x0, waiting for transfers between devices: 89.4 us -> none  [the longest x1 53.8 us: on_device(): lax.psum_scatter(col_sum, 'row', scatter_dimension=1, tiled=True)]
    another operation x126 -> x0, loops' own time: 83.7 us -> none  [the longest x1 45 us: on_device(): lax.fori_loop(0, half_count // group_size, visit_group, (row_start, col_s...]
    dot_general x184 -> x0, matrix products: 74.7 us -> none  [the longest x92 39.3 us: live_terms(): jnp.dot(block_second[7:9], kernel_tile.T, precision=lax.Precision.HIGHEST)]
    ppermute x3 -> x0, starting transfers between devices: 42.2 us -> none  [partner(): return lax.ppermute(block, axis, route)]
    pallas_call x0 -> x3, Pallas kernels: none -> 25.3 us  [the longest x1 21.4 us: pair_terms(): pl.pallas_call(pair_kernel, out_shape=jax.ShapeDtypeStruct((devices * clu...]
    dynamic_slice x48 -> x0, local copies, waits for them, and re-layouts: 22.2 us -> none  [the longest x16 10.3 us: visit_group(): diagonal_all[slot_index] > 0]
    mul x63 -> x0, other arithmetic: 21.9 us -> none  [the longest x40 19.8 us: near_part(): return 0.25 * summed]
  transfers between devices with their start and end apart: 5 -> 2, of which waited for: 3 -> 1; matrix products, arithmetic and copies ran while one was open for 23% -> 0% of each run, Pallas kernels for 0% -> 0%
where the time goes in v1:
time: 241 us; the launch traced here: 240 us
  waiting for transfers between devices  123 us (51%)
  blocking collectives  76.7 us (32%)
  Pallas kernels  25.3 us (10%)
  between operations  13.4 us (6%)
    unnamed x3, waiting for transfers between devices  123 us
    all_gather x1, blocking collectives, on_device(): extra_all = lax.all_gather(extra, ('row', 'col'))  76.7 us
    pallas_call x1, Pallas kernels, pair_terms(): pl.pallas_call(pair_kernel, out_shape=jax.ShapeDtypeStruct((devices * clu...  21.4 us
  transfers between devices with their start and end apart: 2, of which 1 were waited for; matrix products, arithmetic and copies ran while one was open for 0% of the time, Pallas kernels for 0%

profile of v1, /device:TPU:0, one launch (start us, length us, event | category | flops | bytes accessed | tf_op | source)
XLA Modules:
  0.0 240.2 jit_solution(3543224084485295622)
XLA Ops:
  6.5 0.0 all-gather.5.cloned.1.call-start
  6.5 2.1 shard_map.82
  8.7 0.0 copy-start
  8.7 0.0 all-gather.5.cloned.1.call-update
  8.7 0.0 all-reduce.3.cloned.1.call-start
  8.8 0.6 copy-done
  9.4 76.7 %all-gather.2.extra = f32[32,4,512]{2,1,0:T(4,128)} all-gather(f32[1,4,512]{2,1,0:T(4,128)S(1)} %bitcast.10), channel_id=3, replica_groups=mesh['row'=8,'col'=4] {'row','col'}, dimensions={0}, use_global_device_ids=true | all-gather | bytes 270336 | tf_op jit(solution)/shard_map/all_gather | solution.py:264
  86.1 0.0 all-gather.5.cloned.1.call-done
  86.1 21.4 %shard_map.83 = f32[64,2,512]{2,1,0:T(2,128)} custom-call(f32[32,2,8,512]{3,2,1,0:T(8,128)} %bitcast.7, f32[32,4,512]{2,1,0:T(4,128)} %all-gather.2.extra), custom_call_target="tpu_custom_call" | custom-call | tf_op jit(solution)/shard_map/pallas_call | solution.py:220
  107.5 0.0 all-reduce.3.cloned.1.call-update
  107.5 122.7 %all-reduce.3.cloned.1.call-done = f32[64,2,512]{2,1,0:T(2,128)} async-done(((f32[64,2,512]{2,1,0:T(2,128)}), f32[64,2,512]{2,1,0:T(2,128)}) %all-reduce.3.cloned.1.call-update) | async-done | bytes 262160
  230.2 1.3 constant_dynamic-slice_fusion.owned
  231.5 1.8 shard_map.84
Async XLA Ops:
  6.5 79.6 %all-gather.5.cloned.1.call-start = ((), (), s32[]{:S(2)}) async-start(), calls=%async_computation | async-start | bytes 1081344 | tf_op jit(solution)/shard_map/all_gather | solution.py:263
  8.7 0.7 copy-start
  8.7 221.5 %all-reduce.3.cloned.1.call-start = ((), (), s32[]{:S(2)}) async-start(), calls=%async_computation.1 | async-start | bytes 524288
Sparse Core Ops, SparseCore 0:
  10.3 56.5 all-gather.4
  107.6 122.5 all-reduce.2

commit v2 on v1

--- a/solution.py
+++ b/solution.py
@@ -256,14 +256,189 @@
     )(owned, resist[None, :], currents, slot_of[None, :])
 
 
+def greet(barrier, peers):
+    for row, col in peers:
+        pl.semaphore_signal(
+            barrier, inc=1, device_id={"row": row, "col": col}, device_id_type=MESH
+        )
+    pl.semaphore_wait(barrier, len(peers))
+
+
+def gather_kernel(main, extra, main_all, extra_all, send_sem, recv_sem, own_sem):
+    row_count, col_count = lax.axis_size("row"), lax.axis_size("col")
+    row, col = lax.axis_index("row"), lax.axis_index("col")
+    me = row * col_count + col
+    chips = row_count // 2
+    other = row + 1 - 2 * lax.rem(row, 2)
+    gathered = (main_all, extra_all)
+
+    def row_at(base, step):
+        return lax.rem(base + 2 * step, row_count)
+
+    def col_at(step):
+        return lax.rem(col + step, col_count)
+
+    greet(
+        pltpu.get_barrier_semaphore(),
+        [(row, col_at(k)) for k in range(1, col_count)]
+        + [(row_at(row, k), col) for k in range(1, chips)]
+        + [(other, col)],
+    )
+    own = [
+        pltpu.make_async_copy(source, target.at[me], own_sem.at[part])
+        for part, (source, target) in enumerate(zip((main, extra), gathered))
+    ]
+    for copy in own:
+        copy.start()
+
+    def copies(origin, lane, to_row, to_col, mine=False):
+        return [
+            pltpu.make_async_remote_copy(
+                src_ref=source if mine else target.at[origin],
+                dst_ref=target.at[origin],
+                send_sem=send_sem.at[part, lane],
+                recv_sem=recv_sem.at[part, origin],
+                device_id={"row": to_row, "col": to_col},
+                device_id_type=MESH,
+            )
+            for part, (source, target) in enumerate(zip((main, extra), gathered))
+        ]
+
+    sent = []
+
+    def push(origin, to_row, to_col, mine=False):
+        started = copies(origin, len(sent), to_row, to_col, mine)
+        for copy in started:
+            copy.start()
+        sent.append(started)
+
+    def arrive(origin):
+        for copy in copies(origin, 0, other, col):
+            copy.wait_recv()
+
+    def fan_out(origin, mine=False):
+        for k in range(1, chips):
+            push(origin, row_at(row, k), col, mine)
+        push(origin, other, col, mine)
+
+    for k in range(1, col_count):
+        push(me, row, col_at(k), True)
+    fan_out(me, True)
+    for k in range(1, col_count):
+        origin = row * col_count + col_at(col_count - k)
+        arrive(origin)
+        fan_out(origin)
+    for block in range(col_count):
+        for k in range(1, chips):
+            origin = row_at(row, chips - k) * col_count + col_at(col_count - block)
+            arrive(origin)
+            push(origin, other, col)
+    for block in range(col_count):
+        for k in range(chips):
+            arrive(row_at(other, chips - k) * col_count + col_at(col_count - block))
+    for started in sent:
+        for copy in started:
+            copy.wait_send()
+    for copy in own:
+        copy.wait()
+
+
+def gather_all(main, extra):
+    row_count, col_count = lax.axis_size("row"), lax.axis_size("col")
+    devices = row_count * col_count
+    lanes = col_count - 1 + col_count * (row_count - 1)
+    return pl.pallas_call(
+        gather_kernel,
+        out_shape=(
+            jax.ShapeDtypeStruct((devices,) + main.shape, F32),
+            jax.ShapeDtypeStruct((devices,) + extra.shape, F32),
+        ),
+        in_specs=[VMEM, VMEM],
+        out_specs=(VMEM, VMEM),
+        scratch_shapes=[
+            pltpu.SemaphoreType.DMA((2, lanes)),
+            pltpu.SemaphoreType.DMA((2, devices)),
+            pltpu.SemaphoreType.DMA((2,)),
+        ],
+        compiler_params=pltpu.CompilerParams(collective_id=0, has_side_effects=True),
+    )(main, extra)
+
+
+def scatter_kernel(total, owned, arrived, send_sem, recv_sem):
+    row_count, col_count = lax.axis_size("row"), lax.axis_size("col")
+    devices = row_count * col_count
+    clusters = owned.shape[0]
+    me = lax.axis_index("row") * col_count + lax.axis_index("col")
+    barrier = pltpu.get_barrier_semaphore()
+
+    def call_on(step, _):
+        peer = lax.rem(me + step, devices)
+        pl.semaphore_signal(
+            barrier,
+            inc=1,
+            device_id={"row": peer // col_count, "col": lax.rem(peer, col_count)},
+            device_id_type=MESH,
+        )
+        return 0
+
+    lax.fori_loop(1, devices, call_on, 0)
+    pl.semaphore_wait(barrier, devices - 1)
+
+    def copy_of(step):
+        peer = lax.rem(me + step, devices)
+        return pltpu.make_async_remote_copy(
+            src_ref=total.at[pl.ds(peer * clusters, clusters)],
+            dst_ref=arrived.at[step],
+            send_sem=send_sem.at[step],
+            recv_sem=recv_sem.at[step],
+            device_id={"row": peer // col_count, "col": lax.rem(peer, col_count)},
+            device_id_type=MESH,
+        )
+
+    def begin(step, _):
+        copy_of(step).start()
+        return 0
+
+    lax.fori_loop(1, devices, begin, 0)
+    owned[...] = total[pl.ds(me * clusters, clusters)]
+
+    def collect(step, _):
+        copy_of(step).wait_recv()
+        owned[...] += arrived[step]
+        return 0
+
+    lax.fori_loop(1, devices, collect, 0)
+
+    def end(step, _):
+        copy_of(step).wait_send()
+        return 0
+
+    lax.fori_loop(1, devices, end, 0)
+
+
+def scatter_sum(total, clusters):
+    devices = lax.axis_size("row") * lax.axis_size("col")
+    return pl.pallas_call(
+        scatter_kernel,
+        out_shape=jax.ShapeDtypeStruct((clusters,) + total.shape[1:], F32),
+        in_specs=[VMEM],
+        out_specs=VMEM,
+        scratch_shapes=[
+            pltpu.VMEM((devices, clusters) + total.shape[1:], F32),
+            pltpu.SemaphoreType.DMA((devices,)),
+            pltpu.SemaphoreType.DMA((devices,)),
+        ],
+        compiler_params=pltpu.CompilerParams(collective_id=1, has_side_effects=True),
+    )(total)
+
+
 def on_device(positions, segments, radius, currents, resist, slot_of, pair_list, near_flag):
     main, extra = order_elements(
         positions, segments, radius, currents, slot_of, pair_list, near_flag
     )
-    main_all = lax.all_gather(main, ("row", "col"))
-    extra_all = lax.all_gather(extra, ("row", "col"))
+    main_all, extra_all = gather_all(main, extra)
     total = pair_terms(main_all, extra_all)
-    owned = lax.psum_scatter(total, ("row", "col"), scatter_dimension=0, tiled=True)
+    owned = scatter_sum(total, main.shape[0])
     return finish(owned, resist, currents, slot_of)
 
 

time: 241 us -> 59.5 us (0.25)
  waiting for transfers between devices: 123 us -> 0 us
  blocking collectives: 76.7 us -> 0 us
  Pallas kernels: 25.3 us -> 59.2 us
  between operations: 13.4 us -> 0.02 us
    unnamed x3 -> x0, waiting for transfers between devices: 123 us -> none
    all_gather x1 -> x0, blocking collectives: 76.7 us -> none  [on_device(): extra_all = lax.all_gather(extra, ('row', 'col'))]
    pallas_call x0 -> x2, Pallas kernels: none -> 31.4 us  [the longest x1 18.9 us: gather_all(): pl.pallas_call(gather_kernel, out_shape=(jax.ShapeDtypeStruct((devices,)...]
    pallas_call x1, Pallas kernels: 21.4 us -> 23.9 us  [pair_terms(): pl.pallas_call(pair_kernel, out_shape=jax.ShapeDtypeStruct((devices * clu...]
  transfers between devices with their start and end apart: 2 -> 0, of which waited for: 1 -> 0; matrix products, arithmetic and copies ran while one was open for 0% -> 0% of each run, Pallas kernels for 0% -> 0%
where the time goes in v2:
time: 59.5 us; the launch traced here: 59.2 us
  Pallas kernels  59.2 us (99%)
    pallas_call x1, Pallas kernels, pair_terms(): pl.pallas_call(pair_kernel, out_shape=jax.ShapeDtypeStruct((devices * clu...  23.9 us
    pallas_call x1, Pallas kernels, gather_all(): pl.pallas_call(gather_kernel, out_shape=(jax.ShapeDtypeStruct((devices,)...  18.9 us
    pallas_call x1, Pallas kernels, scatter_sum(): pl.pallas_call(scatter_kernel, out_shape=jax.ShapeDtypeStruct((clusters,)...  12.5 us
    pallas_call x1, Pallas kernels, order_elements(): pl.pallas_call(order_kernel, out_shape=(jax.ShapeDtypeStruct((clusters, 8...  2.14 us
    pallas_call x1, Pallas kernels, finish(): pl.pallas_call(finish_kernel, out_shape=jax.ShapeDtypeStruct(currents.sha...  1.78 us

profile of v2, /device:TPU:0, one launch (start us, length us, event | category | flops | bytes accessed | tf_op | source)
XLA Modules:
  0.0 59.2 jit_solution(2262144968116419841)
XLA Ops:
  0.0 2.1 %shard_map.82 = (f32[2,8,512]{2,1,0:T(8,128)}, f32[4,512]{1,0:T(4,128)}) custom-call(f32[3,1024]{1,0:T(4,128)} %pos.1, f32[3,1024]{1,0:T(4,128)} %seg.1, f32[1,1024]{1,0:T(1,128)} %bitcast.7, f32[2,1024]{1,0:T(2,128)} %cur.3, s32[1,1024]{1,0:T(1,128)} %bitcast.5, s32[2,32]{1,0:T(2,128)} %bitcast.9, s32[1,32]{1,0:T(1,128)} %bitcast.10), custom_call_target="tpu_custom_call" | custom-call | tf_op jit(solution)/shard_map/pallas_call | solution.py:65
  2.1 18.9 %shard_map.83 = (f32[32,2,8,512]{3,2,1,0:T(8,128)}, f32[32,4,512]{2,1,0:T(4,128)}) custom-call(f32[2,8,512]{2,1,0:T(8,128)} %get-tuple-element.9.main, f32[4,512]{1,0:T(4,128)} %get-tuple-element.10.extra), custom_call_target="tpu_custom_call" | custom-call | tf_op jit(solution)/shard_map/pallas_call | solution.py:350
  21.1 23.9 %shard_map.84.total = f32[64,2,512]{2,1,0:T(2,128)} custom-call(f32[32,2,8,512]{3,2,1,0:T(8,128)} %get-tuple-element.11.main, f32[32,4,512]{2,1,0:T(4,128)} %get-tuple-element.12.extra), custom_call_target="tpu_custom_call" | custom-call | tf_op jit(solution)/shard_map/pallas_call | solution.py:220
  44.9 12.5 %shard_map.85.owned = f32[2,2,512]{2,1,0:T(2,128)} custom-call(f32[64,2,512]{2,1,0:T(2,128)} %shard_map.84.total), custom_call_target="tpu_custom_call" | custom-call | tf_op jit(solution)/shard_map/pallas_call | solution.py:421
  57.4 1.8 %shard_map.86 = f32[2,1024]{1,0:T(2,128)} custom-call(f32[2,2,512]{2,1,0:T(2,128)} %shard_map.85.owned, f32[1,1024]{1,0:T(1,128)} %bitcast.8, f32[2,1024]{1,0:T(2,128)} %cur.3, s32[1,1024]{1,0:T(1,128)} %bitcast.6), custom_call_target="tpu_custom_call" | custom-call | tf_op jit(solution)/shard_map/pallas_call | solution.py:250

commit v3 on v2

--- a/solution.py
+++ b/solution.py
@@ -15,7 +15,9 @@
 gauss_step = 0.5 / math.sqrt(3.0)
 kernel_gain = 0.25
 VMEM = pl.BlockSpec(memory_space=pltpu.VMEM)
-CHUNK = 256
+TALL = 256
+WIDE = 512
+FAR = 2
 
 
 def split_three(value):
@@ -88,8 +90,9 @@
     total[...] = jnp.zeros_like(total)
     for feat, ones in ((feat_first, 21), (feat_second, 18)):
         feat[...] = jnp.zeros_like(feat)
-        for sign in range(2):
-            feat[sign, ones : ones + 3, :] = jnp.ones((3, CS), F32)
+        for unit in range(FAR):
+            for sign in range(2):
+                feat[unit, sign, ones : ones + 3, :] = jnp.ones((3, CS), F32)
     weight_first[...] = jnp.zeros_like(weight_first)
     weight_second[...] = jnp.zeros_like(weight_second)
 
@@ -122,7 +125,10 @@
         rank_in(is_near),
         jnp.where(is_far > 0.5, rank_in(is_far) + near_count, -1.0),
     ).astype(jnp.int32)
-    mine = (live_count.astype(jnp.int32) + (devices - 1 - me)) // devices
+    def share(count):
+        return (count.astype(jnp.int32) + (devices - 1 - me)) // devices
+
+    mine_near, mine = share(near_count), share(live_count)
 
     def pick(turn):
         found = jnp.where(rank == turn * devices + me, code, 0.0)
@@ -132,7 +138,6 @@
         device, local = cluster // clusters, cluster % clusters
         block = main[device, local]
         imag = extra[device, pl.ds(local, 1), :]
-        wide = []
         for axis in range(3):
             vector = block[3 + axis : 4 + axis]
             for part, current in enumerate((block[7:8], imag)):
@@ -143,21 +148,13 @@
                 weights[8 + row : 9 + row, :] = product - high
         return block
 
-    def write_first(sign, points, radii):
+    def write(feat, points, radii, gain, order, norm_row):
         norm = jnp.sum(points * points, axis=0, keepdims=True) + radii * radii
-        high, middle, low = split_three(points)
-        for slot, piece in enumerate((high, high, middle, middle, high, low)):
-            feat_first[sign, 3 * slot : 3 * slot + 3, :] = piece
+        parts = split_three(gain * points)
+        for slot, part in enumerate(order):
+            feat[3 * slot : 3 * slot + 3, :] = parts[part]
         for row, piece in enumerate(split_three(norm)):
-            feat_first[sign, 18 + row : 19 + row, :] = piece
-
-    def write_second(sign, points, radii):
-        norm = jnp.sum(points * points, axis=0, keepdims=True) + radii * radii
-        high, middle, low = split_three(-2.0 * points)
-        for slot, piece in enumerate((high, middle, high, middle, low, high)):
-            feat_second[sign, 3 * slot : 3 * slot + 3, :] = piece
-        for row, piece in enumerate(split_three(norm)):
-            feat_second[sign, 21 + row : 22 + row, :] = piece
+            feat[norm_row + row : norm_row + row + 1, :] = piece
 
     def contract(sums, block, scale):
         both = sums[0:8] + sums[8:16]
@@ -166,53 +163,84 @@
             result = result + both[2 * axis : 2 * axis + 2] * block[3 + axis : 4 + axis]
         return result * scale
 
-    def apply(signs, first, second, block_first, block_second, scale):
-        for sign in range(signs):
-            step = (gauss_step if sign else -gauss_step) if signs > 1 else 0.0
-            for block, write in ((block_first, write_first), (block_second, write_second)):
-                points = block[0:3] - 0.5
-                if signs > 1:
-                    points = points + step * block[3:6]
-                write(sign, points, block[6:7])
-        left = [feat_first[sign].T.astype(BF16) for sign in range(signs)]
-        right = [feat_second[sign].astype(BF16) for sign in range(signs)]
-        from_first = weight_first[...].astype(BF16)
-        from_second = weight_second[...].astype(BF16)
-        mirror = jnp.zeros((16, CS), F32)
-        direct = []
-        for start in range(0, CS, CHUNK):
-            inverse = 0.0
-            for one in left:
-                for other in right:
-                    inverse = inverse + lax.rsqrt(dot_nn(one[start : start + CHUNK], other))
-            high = inverse.astype(BF16)
-            low = (inverse - high.astype(F32)).astype(BF16)
-            direct.append(dot_nt(from_second, high) + dot_nt(from_second, low))
-            rows = from_first[:, start : start + CHUNK]
-            mirror = mirror + dot_nn(rows, high) + dot_nn(rows, low)
-        direct = jnp.concatenate(direct, 1)
-        total[first] += contract(direct, block_first, scale)
-        keep = jnp.where(first == second, 0.0, scale)
-        total[second] += contract(mirror, block_second, keep)
-
-    def visit(turn, now):
-        flag = now % 4
-        second = now // 4 % 1024
-        first = now // 4096
-        block_first = load(first, weight_first)
-        block_second = load(second, weight_second)
-
-        @pl.when(flag == 2)
-        def _():
-            apply(2, first, second, block_first, block_second, kernel_gain * 0.25)
-
-        @pl.when(flag != 2)
-        def _():
-            apply(1, first, second, block_first, block_second, kernel_gain)
-
+    def apply(codes_and_scales, signs):
+        units = []
+        for unit, (now, scale) in enumerate(codes_and_scales):
+            first, second = now // 4096, now // 4 % 1024
+            block_first = load(first, weight_first.at[unit])
+            block_second = load(second, weight_second.at[unit])
+            for sign in range(signs):
+                step = gauss_step if sign else -gauss_step
+                for block, feat, gain, order, norm_row in (
+                    (block_first, feat_first, 1.0, (0, 0, 1, 1, 0, 2), 18),
+                    (block_second, feat_second, -2.0, (0, 1, 0, 1, 2, 0), 21),
+                ):
+                    points = block[0:3] - 0.5
+                    if signs > 1:
+                        points = points + step * block[3:6]
+                    write(feat.at[unit, sign], points, block[6:7], gain, order, norm_row)
+            units.append((unit, first, second, block_first, block_second, scale))
+        sides = []
+        for unit, *_ in units:
+            left = [feat_first[unit, sign].T.astype(BF16) for sign in range(signs)]
+            right = [feat_second[unit, sign].astype(BF16) for sign in range(signs)]
+            from_first = weight_first[unit].astype(BF16)
+            turned = weight_second[unit].T.astype(BF16)
+            sides.append((left, right, from_first, turned))
+        mirrors = [[0.0 for _ in range(0, CS, WIDE)] for _ in units]
+        directs = [[] for _ in units]
+        for start in range(0, CS, TALL):
+            sums = [0.0 for _ in units]
+            for index, across in enumerate(range(0, CS, WIDE)):
+                for unit, (left, right, from_first, turned) in enumerate(sides):
+                    inverse = 0.0
+                    for one in left:
+                        for other in right:
+                            inverse = inverse + lax.rsqrt(
+                                dot_nn(one[start : start + TALL], other[:, across : across + WIDE])
+                            )
+                    high = inverse.astype(BF16)
+                    low = (inverse - high.astype(F32)).astype(BF16)
+                    near_side = turned[across : across + WIDE]
+                    rows = from_first[:, start : start + TALL]
+                    sums[unit] = sums[unit] + dot_nn(high, near_side) + dot_nn(low, near_side)
+                    mirrors[unit][index] = (
+                        mirrors[unit][index] + dot_nn(rows, high) + dot_nn(rows, low)
+                    )
+            for unit, _ in enumerate(units):
+                directs[unit].append(sums[unit])
+        terms = []
+        for unit, first, second, block_first, block_second, scale in units:
+            direct = jnp.concatenate(directs[unit], 0).T
+            mirror = jnp.concatenate(mirrors[unit], 1)
+            keep = jnp.where(first == second, 0.0, scale)
+            terms.append((first, contract(direct, block_first, scale)))
+            terms.append((second, contract(mirror, block_second, keep)))
+        for cluster, term in terms:
+            total[cluster] += term
+
+    def visit_near(turn, now):
+        apply([(now, kernel_gain * 0.25)], 2)
         return pick(turn + 1)
 
-    lax.fori_loop(0, mine, visit, pick(0))
+    def visit_far(step, codes):
+        turn = mine_near + FAR * step
+        apply(
+            [
+                (now, kernel_gain if unit == 0 else jnp.where(turn + unit < mine, kernel_gain, 0.0))
+                for unit, now in enumerate(codes)
+            ],
+            1,
+        )
+        return tuple(pick(turn + FAR + unit) for unit in range(FAR))
+
+    start = lax.fori_loop(0, mine_near, visit_near, pick(0))
+    lax.fori_loop(
+        0,
+        (mine - mine_near + FAR - 1) // FAR,
+        visit_far,
+        (start,) + tuple(pick(mine_near + unit) for unit in range(1, FAR)),
+    )
 
 
 def pair_terms(main, extra):
@@ -223,10 +251,10 @@
         in_specs=[VMEM, VMEM],
         out_specs=VMEM,
         scratch_shapes=[
-            pltpu.VMEM((2, 32, CS), F32),
-            pltpu.VMEM((2, 32, CS), F32),
-            pltpu.VMEM((16, CS), F32),
-            pltpu.VMEM((16, CS), F32),
+            pltpu.VMEM((FAR, 2, 32, CS), F32),
+            pltpu.VMEM((FAR, 2, 32, CS), F32),
+            pltpu.VMEM((FAR, 16, CS), F32),
+            pltpu.VMEM((FAR, 16, CS), F32),
         ],
     )(main, extra)
 

time: 59.5 us -> 54.6 us (0.918)
  Pallas kernels: 59.2 us -> 54.3 us
    pallas_call x1, Pallas kernels: 23.9 us -> 17.8 us  [pair_terms(): pl.pallas_call(pair_kernel, out_shape=jax.ShapeDtypeStruct((devices * clu...]
    pallas_call x1, Pallas kernels: 12.5 us -> 13.6 us  [scatter_sum(): pl.pallas_call(scatter_kernel, out_shape=jax.ShapeDtypeStruct((clusters,)...]
where the time goes in v3:
time: 54.6 us; the launch traced here: 54.3 us
  Pallas kernels  54.3 us (99%)
    pallas_call x1, Pallas kernels, gather_all(): pl.pallas_call(gather_kernel, out_shape=(jax.ShapeDtypeStruct((devices,)...  18.9 us
    pallas_call x1, Pallas kernels, pair_terms(): pl.pallas_call(pair_kernel, out_shape=jax.ShapeDtypeStruct((devices * clu...  17.8 us
    pallas_call x1, Pallas kernels, scatter_sum(): pl.pallas_call(scatter_kernel, out_shape=jax.ShapeDtypeStruct((clusters,)...  13.6 us
    pallas_call x1, Pallas kernels, order_elements(): pl.pallas_call(order_kernel, out_shape=(jax.ShapeDtypeStruct((clusters, 8...  2.14 us
    pallas_call x1, Pallas kernels, finish(): pl.pallas_call(finish_kernel, out_shape=jax.ShapeDtypeStruct(currents.sha...  1.78 us

profile of v3, /device:TPU:0, one launch (start us, length us, event | category | flops | bytes accessed | tf_op | source)
XLA Modules:
  0.0 54.3 jit_solution(9347748334288046967)
XLA Ops:
  0.0 2.1 %shard_map.82 = (f32[2,8,512]{2,1,0:T(8,128)}, f32[4,512]{1,0:T(4,128)}) custom-call(f32[3,1024]{1,0:T(4,128)} %pos.1, f32[3,1024]{1,0:T(4,128)} %seg.1, f32[1,1024]{1,0:T(1,128)} %bitcast.7, f32[2,1024]{1,0:T(2,128)} %cur.3, s32[1,1024]{1,0:T(1,128)} %bitcast.5, s32[2,32]{1,0:T(2,128)} %bitcast.9, s32[1,32]{1,0:T(1,128)} %bitcast.10), custom_call_target="tpu_custom_call" | custom-call | tf_op jit(solution)/shard_map/pallas_call | solution.py:67
  2.1 18.9 %shard_map.83 = (f32[32,2,8,512]{3,2,1,0:T(8,128)}, f32[32,4,512]{2,1,0:T(4,128)}) custom-call(f32[2,8,512]{2,1,0:T(8,128)} %get-tuple-element.9.main, f32[4,512]{1,0:T(4,128)} %get-tuple-element.10.extra), custom_call_target="tpu_custom_call" | custom-call | tf_op jit(solution)/shard_map/pallas_call | solution.py:378
  21.1 17.8 %shard_map.84.total = f32[64,2,512]{2,1,0:T(2,128)} custom-call(f32[32,2,8,512]{3,2,1,0:T(8,128)} %get-tuple-element.11.main, f32[32,4,512]{2,1,0:T(4,128)} %get-tuple-element.12.extra), custom_call_target="tpu_custom_call" | custom-call | tf_op jit(solution)/shard_map/pallas_call | solution.py:248
  38.9 13.6 %shard_map.85.owned = f32[2,2,512]{2,1,0:T(2,128)} custom-call(f32[64,2,512]{2,1,0:T(2,128)} %shard_map.84.total), custom_call_target="tpu_custom_call" | custom-call | tf_op jit(solution)/shard_map/pallas_call | solution.py:449
  52.5 1.8 %shard_map.86 = f32[2,1024]{1,0:T(2,128)} custom-call(f32[2,2,512]{2,1,0:T(2,128)} %shard_map.85.owned, f32[1,1024]{1,0:T(1,128)} %bitcast.8, f32[2,1024]{1,0:T(2,128)} %cur.3, s32[1,1024]{1,0:T(1,128)} %bitcast.6), custom_call_target="tpu_custom_call" | custom-call | tf_op jit(solution)/shard_map/pallas_call | solution.py:278

commit v4 on v3

--- a/solution.py
+++ b/solution.py
@@ -40,7 +40,7 @@
     return jnp.where(rows == slots, 1.0, 0.0).astype(BF16)
 
 
-def order_kernel(pos, seg, rad, cur, slot, pair, flag, main, extra, stack):
+def order_into(pos, seg, rad, cur, slot, pair, flag, main, extra, stack):
     clusters = main.shape[0]
     slots = slot[...]
     stack[...] = jnp.zeros_like(stack)
@@ -59,29 +59,6 @@
     extra[clusters : clusters + 1, 0:listed] = pair[0:1, :].astype(F32)
     extra[clusters : clusters + 1, 128 : 128 + listed] = pair[1:2, :].astype(F32)
     extra[clusters : clusters + 1, 256 : 256 + listed] = flag[...].astype(F32)
-
-
-def order_elements(positions, segments, radius, currents, slot_of, pair_list, near_flag):
-    local = positions.shape[1]
-    clusters = local // CS
-    return pl.pallas_call(
-        order_kernel,
-        out_shape=(
-            jax.ShapeDtypeStruct((clusters, 8, CS), F32),
-            jax.ShapeDtypeStruct((clusters + 2, CS), F32),
-        ),
-        in_specs=[VMEM] * 7,
-        out_specs=(VMEM, VMEM),
-        scratch_shapes=[pltpu.VMEM((48, local), F32)],
-    )(
-        positions,
-        segments,
-        radius[None, :],
-        currents,
-        slot_of[None, :],
-        pair_list.T,
-        near_flag[None, :],
-    )
 
 
 def pair_kernel(main, extra, total, feat_first, feat_second, weight_first, weight_second):
@@ -259,40 +236,9 @@
     )(main, extra)
 
 
-def finish_kernel(owned, resist, cur, slot, out, stack):
-    clusters = owned.shape[0]
-    slots = slot[...]
-    sums = jnp.zeros((16, slots.shape[1]), F32)
-    stack[...] = jnp.zeros_like(stack)
-    for cluster in range(clusters):
-        for part, piece in enumerate(split_three(owned[cluster])):
-            stack[2 * part : 2 * part + 2, :] = piece
-        sums = sums + dot_nn(stack[...].astype(BF16), one_hot_rows(slots, cluster * CS, CS))
-    induced = sums[0:2] + sums[2:4] + sums[4:6]
-    scaled = resist[...] * cur[...]
-    out[0:1, :] = scaled[0:1] - induced[1:2]
-    out[1:2, :] = scaled[1:2] + induced[0:1]
-
-
-def finish(owned, resist, currents, slot_of):
-    return pl.pallas_call(
-        finish_kernel,
-        out_shape=jax.ShapeDtypeStruct(currents.shape, F32),
-        in_specs=[VMEM] * 4,
-        out_specs=VMEM,
-        scratch_shapes=[pltpu.VMEM((16, CS), F32)],
-    )(owned, resist[None, :], currents, slot_of[None, :])
-
-
-def greet(barrier, peers):
-    for row, col in peers:
-        pl.semaphore_signal(
-            barrier, inc=1, device_id={"row": row, "col": col}, device_id_type=MESH
-        )
-    pl.semaphore_wait(barrier, len(peers))
-
-
-def gather_kernel(main, extra, main_all, extra_all, send_sem, recv_sem, own_sem):
+def gather_kernel(
+    pos, seg, rad, cur, slot, pair, flag, main_all, extra_all, stack, send_sem, recv_sem
+):
     row_count, col_count = lax.axis_size("row"), lax.axis_size("col")
     row, col = lax.axis_index("row"), lax.axis_index("col")
     me = row * col_count + col
@@ -306,36 +252,35 @@
     def col_at(step):
         return lax.rem(col + step, col_count)
 
-    greet(
-        pltpu.get_barrier_semaphore(),
-        [(row, col_at(k)) for k in range(1, col_count)]
-        + [(row_at(row, k), col) for k in range(1, chips)]
-        + [(other, col)],
+    barrier = pltpu.get_barrier_semaphore()
+    peers = [(row, col_at(k)) for k in range(1, col_count)]
+    peers += [(row_at(row, k), col) for k in range(1, chips)] + [(other, col)]
+    for to_row, to_col in peers:
+        pl.semaphore_signal(
+            barrier, inc=1, device_id={"row": to_row, "col": to_col}, device_id_type=MESH
+        )
+    order_into(
+        pos, seg, rad, cur, slot, pair, flag, main_all.at[me], extra_all.at[me], stack
     )
-    own = [
-        pltpu.make_async_copy(source, target.at[me], own_sem.at[part])
-        for part, (source, target) in enumerate(zip((main, extra), gathered))
-    ]
-    for copy in own:
-        copy.start()
-
-    def copies(origin, lane, to_row, to_col, mine=False):
+    pl.semaphore_wait(barrier, len(peers))
+
+    def copies(origin, lane, to_row, to_col):
         return [
             pltpu.make_async_remote_copy(
-                src_ref=source if mine else target.at[origin],
+                src_ref=target.at[origin],
                 dst_ref=target.at[origin],
                 send_sem=send_sem.at[part, lane],
                 recv_sem=recv_sem.at[part, origin],
                 device_id={"row": to_row, "col": to_col},
                 device_id_type=MESH,
             )
-            for part, (source, target) in enumerate(zip((main, extra), gathered))
+            for part, target in enumerate(gathered)
         ]
 
     sent = []
 
-    def push(origin, to_row, to_col, mine=False):
-        started = copies(origin, len(sent), to_row, to_col, mine)
+    def push(origin, to_row, to_col):
+        started = copies(origin, len(sent), to_row, to_col)
         for copy in started:
             copy.start()
         sent.append(started)
@@ -344,14 +289,14 @@
         for copy in copies(origin, 0, other, col):
             copy.wait_recv()
 
-    def fan_out(origin, mine=False):
+    def fan_out(origin):
         for k in range(1, chips):
-            push(origin, row_at(row, k), col, mine)
-        push(origin, other, col, mine)
+            push(origin, row_at(row, k), col)
+        push(origin, other, col)
 
     for k in range(1, col_count):
-        push(me, row, col_at(k), True)
-    fan_out(me, True)
+        push(me, row, col_at(k))
+    fan_out(me)
     for k in range(1, col_count):
         origin = row * col_count + col_at(col_count - k)
         arrive(origin)
@@ -367,32 +312,42 @@
     for started in sent:
         for copy in started:
             copy.wait_send()
-    for copy in own:
-        copy.wait()
-
-
-def gather_all(main, extra):
+
+
+def gather_all(positions, segments, radius, currents, slot_of, pair_list, near_flag):
     row_count, col_count = lax.axis_size("row"), lax.axis_size("col")
     devices = row_count * col_count
+    local = positions.shape[1]
+    clusters = local // CS
     lanes = col_count - 1 + col_count * (row_count - 1)
     return pl.pallas_call(
         gather_kernel,
         out_shape=(
-            jax.ShapeDtypeStruct((devices,) + main.shape, F32),
-            jax.ShapeDtypeStruct((devices,) + extra.shape, F32),
+            jax.ShapeDtypeStruct((devices, clusters, 8, CS), F32),
+            jax.ShapeDtypeStruct((devices, clusters + 2, CS), F32),
         ),
-        in_specs=[VMEM, VMEM],
+        in_specs=[VMEM] * 7,
         out_specs=(VMEM, VMEM),
         scratch_shapes=[
+            pltpu.VMEM((48, local), F32),
             pltpu.SemaphoreType.DMA((2, lanes)),
             pltpu.SemaphoreType.DMA((2, devices)),
-            pltpu.SemaphoreType.DMA((2,)),
         ],
         compiler_params=pltpu.CompilerParams(collective_id=0, has_side_effects=True),
-    )(main, extra)
-
-
-def scatter_kernel(total, owned, arrived, send_sem, recv_sem):
+    )(
+        positions,
+        segments,
+        radius[None, :],
+        currents,
+        slot_of[None, :],
+        pair_list.T,
+        near_flag[None, :],
+    )
+
+
+def scatter_kernel(
+    total, resist, cur, slot, out, owned, arrived, chosen, stack, send_sem, recv_sem
+):
     row_count, col_count = lax.axis_size("row"), lax.axis_size("col")
     devices = row_count * col_count
     clusters = owned.shape[0]
@@ -410,6 +365,10 @@
         return 0
 
     lax.fori_loop(1, devices, call_on, 0)
+    slots = slot[...]
+    for cluster in range(clusters):
+        chosen[cluster] = one_hot_rows(slots, cluster * CS, CS)
+    stack[...] = jnp.zeros_like(stack)
     pl.semaphore_wait(barrier, devices - 1)
 
     def copy_of(step):
@@ -436,6 +395,15 @@
         return 0
 
     lax.fori_loop(1, devices, collect, 0)
+    sums = jnp.zeros((16, slots.shape[1]), F32)
+    for cluster in range(clusters):
+        for part, piece in enumerate(split_three(owned[cluster])):
+            stack[2 * part : 2 * part + 2, :] = piece
+        sums = sums + dot_nn(stack[...].astype(BF16), chosen[cluster])
+    induced = sums[0:2] + sums[2:4] + sums[4:6]
+    scaled = resist[...] * cur[...]
+    out[0:1, :] = scaled[0:1] - induced[1:2]
+    out[1:2, :] = scaled[1:2] + induced[0:1]
 
     def end(step, _):
         copy_of(step).wait_send()
@@ -444,30 +412,33 @@
     lax.fori_loop(1, devices, end, 0)
 
 
-def scatter_sum(total, clusters):
+def scatter_finish(total, resist, currents, slot_of):
     devices = lax.axis_size("row") * lax.axis_size("col")
+    local = currents.shape[1]
+    clusters = local // CS
     return pl.pallas_call(
         scatter_kernel,
-        out_shape=jax.ShapeDtypeStruct((clusters,) + total.shape[1:], F32),
-        in_specs=[VMEM],
+        out_shape=jax.ShapeDtypeStruct(currents.shape, F32),
+        in_specs=[VMEM] * 4,
         out_specs=VMEM,
         scratch_shapes=[
+            pltpu.VMEM((clusters,) + total.shape[1:], F32),
             pltpu.VMEM((devices, clusters) + total.shape[1:], F32),
+            pltpu.VMEM((clusters, CS, local), BF16),
+            pltpu.VMEM((16, CS), F32),
             pltpu.SemaphoreType.DMA((devices,)),
             pltpu.SemaphoreType.DMA((devices,)),
         ],
         compiler_params=pltpu.CompilerParams(collective_id=1, has_side_effects=True),
-    )(total)
+    )(total, resist[None, :], currents, slot_of[None, :])
 
 
 def on_device(positions, segments, radius, currents, resist, slot_of, pair_list, near_flag):
-    main, extra = order_elements(
+    main_all, extra_all = gather_all(
         positions, segments, radius, currents, slot_of, pair_list, near_flag
     )
-    main_all, extra_all = gather_all(main, extra)
     total = pair_terms(main_all, extra_all)
-    owned = scatter_sum(total, main.shape[0])
-    return finish(owned, resist, currents, slot_of)
+    return scatter_finish(total, resist, currents, slot_of)
 
 
 def solution(mesh):

time: 54.6 us -> 52.4 us (0.960)
  Pallas kernels: 54.3 us -> 50.9 us
  local copies, waits for them, and re-layouts: 0 us -> 1.3 us
    pallas_call x4 -> x2, Pallas kernels: 36.5 us -> 33 us  [the longest x1 19 us: gather_all(): pl.pallas_call(gather_kernel, out_shape=(jax.ShapeDtypeStruct((devices, c...]
    unnamed x0 -> x1, local copies, waits for them, and re-layouts: none -> 1.3 us
where the time goes in v4:
time: 52.4 us; the launch traced here: 52.2 us
  Pallas kernels  50.9 us (97%)
  local copies, waits for them, and re-layouts  1.3 us (2%)
    pallas_call x1, Pallas kernels, gather_all(): pl.pallas_call(gather_kernel, out_shape=(jax.ShapeDtypeStruct((devices, c...  19 us
    pallas_call x1, Pallas kernels, pair_terms(): pl.pallas_call(pair_kernel, out_shape=jax.ShapeDtypeStruct((devices * clu...  17.8 us
    pallas_call x1, Pallas kernels, scatter_finish(): pl.pallas_call(scatter_kernel, out_shape=jax.ShapeDtypeStruct(currents.sh...  14.1 us
    unnamed x1, local copies, waits for them, and re-layouts  1.3 us

profile of v4, /device:TPU:0, one launch (start us, length us, event | category | flops | bytes accessed | tf_op | source)
XLA Modules:
  0.0 52.2 jit_solution(119233215152020602)
XLA Ops:
  0.0 19.0 %shard_map.82 = (f32[32,2,8,512]{3,2,1,0:T(8,128)}, f32[32,4,512]{2,1,0:T(4,128)}) custom-call(f32[3,1024]{1,0:T(4,128)} %pos.1, f32[3,1024]{1,0:T(4,128)} %seg.1, f32[1,1024]{1,0:T(1,128)} %bitcast.8, f32[2,1024]{1,0:T(2,128)} %cur.3, s32[1,1024]{1,0:T(1,128)} %bitcast.5, s32[2,32]{1,0:T(2,128)} %bitcast.9, s32[1,32]{1,0:T(1,128)} %bitcast.10), custom_call_target="tpu_custom_call" | custom-call | tf_op jit(solution)/shard_map/pallas_call | solution.py:323
  19.0 17.8 %shard_map.83.total = f32[64,2,512]{2,1,0:T(2,128)} custom-call(f32[32,2,8,512]{3,2,1,0:T(8,128)} %get-tuple-element.7.main, f32[32,4,512]{2,1,0:T(4,128)} %get-tuple-element.8.extra), custom_call_target="tpu_custom_call" | custom-call | tf_op jit(solution)/shard_map/pallas_call | solution.py:225
  36.8 14.1 %shard_map.84 = f32[2,1024]{1,0:T(2,128)} custom-call(f32[64,2,512]{2,1,0:T(2,128)} %shard_map.83.total, f32[1,1024]{1,0:T(1,128)} %bitcast.7, f32[2,1024]{1,0:T(2,128)} %cur.3, s32[1,1024]{1,0:T(1,128)} %bitcast.6), custom_call_target="tpu_custom_call" | custom-call | tf_op jit(solution)/shard_map/pallas_call | solution.py:419
  50.9 1.3 %copy.10 = f32[2,1024]{1,0:T(2,128)} copy(f32[2,1024]{1,0:T(2,128)} %shard_map.84) | data formatting | bytes 16384
